TPU v7x, 128 devices: a whole 4x4x4 slice. The times are simulated.
128 devices in a mesh: expert: 4 (over z), seq: 4 (over y), tensor: 8 (over x, core).
Axes of the slice: x: 4, y: 4, z: 4, core: 2. Of those that a mesh axis runs over, the one named last changes fastest.
Arguments:
- tokens: bfloat16 [3072, 7168], P(('expert', 'seq')), may hold values from -6 to 6
- grad_out: bfloat16 [3072, 7168], P(('expert', 'seq')), may hold values from -6 to 6
- expert_ids: int32 [3072, 2], P(('expert', 'seq')), may hold values from 0 to 3, all different within a row; in each aligned block of 192 rows (0 to 191, 192 to 383, ...) at most 128 rows name the same one
- route_weights: bfloat16 [3072, 2], P(('expert', 'seq')), may hold values from 0.099609375 to 1
- gate_weight: bfloat16 [4, 7168, 2048], P('expert', 'seq', 'tensor'), may hold values from -0.0625 to 0.0625
- up_weight: bfloat16 [4, 7168, 2048], P('expert', 'seq', 'tensor'), may hold values from -0.0625 to 0.0625
- down_weight: bfloat16 [4, 7168, 2048], P('expert', 'seq', 'tensor'), may hold values from -0.125 to 0.125
Outputs:
- grad_tokens: bfloat16 [3072, 7168], P(('expert', 'seq'), 'tensor')
- grad_route: float32 [3072, 2], P(('expert', 'seq'))
- grad_gate: float32 [4, 7168, 2048], P('expert', 'seq', 'tensor')
- grad_up: float32 [4, 7168, 2048], P('expert', 'seq', 'tensor')
- grad_down: float32 [4, 7168, 2048], P('expert', 'seq', 'tensor')
Inputs may be any that keep to these rules, and one draw needn't show every extreme that they name: `expert_ids`: the two ids of a row differ. Within each aligned block of 192 rows (the tokens of one group of the expert and seq axes) no expert is named by more than 128 rows, and in some block an expert is named by exactly 128 rows.
All inputs are finite; a program needn't handle non-finite values.
Results may differ from a plain program's by a relative error of at most 0.019.
Values may be sent and summed in bfloat16 or wider, within the bound.
A program may use at most 192 MiB of HBM per device.

v0:
```python
import jax
import jax.numpy as jnp
from jax import lax
from jax.sharding import PartitionSpec as P


def shards(tokens, grad_out, expert_ids, route_weights, gate_weight, up_weight, down_weight):
    expert_count = lax.axis_size("expert")
    seq_count = lax.axis_size("seq")
    tensor_count = lax.axis_size("tx") * lax.axis_size("core")
    core = lax.axis_index("core")
    local_count = gate_weight.shape[0]
    tok_rows = tokens.shape[0]
    model_width = tokens.shape[1]
    part_width = model_width // tensor_count
    per_peer = tok_rows // 6
    peer_count = expert_count * seq_count
    block_rows = local_count * per_peer
    slot_count = peer_count * block_rows
    flat_ids = expert_ids.reshape(-1)
    route_count = flat_ids.shape[0]
    onehot = (
        flat_ids[:, None] == jnp.arange(local_count * expert_count, dtype=jnp.int32)[None, :]
    ).astype(jnp.int32)
    before = jnp.cumsum(onehot, axis=0) - onehot
    ranking = jnp.sum(before * onehot, axis=1)
    local_expert = flat_ids % local_count
    dest_peer = flat_ids // local_count * seq_count + ranking % seq_count
    target = (dest_peer * local_count + local_expert) * per_peer + ranking // seq_count
    source = (
        jnp.full((slot_count,), -1, jnp.int32)
        .at[target]
        .set(jnp.arange(route_count, dtype=jnp.int32))
    )
    filled = source >= 0
    safe_source = jnp.maximum(source, 0)
    token_of = safe_source // 2
    keep = filled[:, None].astype(tokens.dtype)
    weight_send = (
        route_weights.reshape(-1)[safe_source] * filled.astype(route_weights.dtype)
    ).reshape(peer_count, block_rows)
    half = model_width // 2
    tokens_half = lax.dynamic_slice_in_dim(tokens, core * half, half, axis=1)
    grad_half = lax.dynamic_slice_in_dim(grad_out, core * half, half, axis=1)
    in_send = (tokens_half[token_of] * keep).reshape(peer_count, block_rows, half)
    out_send = (grad_half[token_of] * keep).reshape(peer_count, block_rows, half)
    in_mine, out_mine, weight_recv = (
        lax.all_to_all(in_send, ("expert", "seq"), split_axis=0, concat_axis=0, tiled=True),
        lax.all_to_all(out_send, ("expert", "seq"), split_axis=0, concat_axis=0, tiled=True),
        lax.all_to_all(weight_send, ("expert", "seq"), split_axis=0, concat_axis=0, tiled=True),
    )

    def join_halves(mine):
        other = lax.ppermute(mine, "core", [(0, 1), (1, 0)])
        first = jnp.where(core == 0, mine, other)
        second = jnp.where(core == 0, other, mine)
        return jnp.concatenate([first, second], axis=-1)

    in_recv = join_halves(in_mine)
    out_recv = join_halves(out_mine)

    def by_expert(values):
        shaped = values.reshape((peer_count, local_count, per_peer) + values.shape[2:])
        return jnp.swapaxes(shaped, 0, 1).reshape(
            (local_count, peer_count * per_peer) + values.shape[2:]
        )

    def by_peer(values):
        shaped = values.reshape((local_count, peer_count, per_peer) + values.shape[2:])
        return jnp.swapaxes(shaped, 0, 1).reshape((peer_count, block_rows) + values.shape[2:])

    in_rows = by_expert(in_recv)
    out_rows = by_expert(out_recv)
    prob = by_expert(weight_recv).astype(jnp.float32)[:, :, None]
    gate_full, up_full, down_full = (
        lax.all_gather(gate_weight, "seq", axis=1, tiled=True),
        lax.all_gather(up_weight, "seq", axis=1, tiled=True),
        lax.all_gather(down_weight, "seq", axis=1, tiled=True),
    )
    pre_gate = jnp.einsum("emd,edf->emf", in_rows, gate_full, preferred_element_type=jnp.float32)
    pre_up = jnp.einsum("emd,edf->emf", in_rows, up_full, preferred_element_type=jnp.float32)
    sigmoid_gate = jax.nn.sigmoid(pre_gate)
    silu_gate = pre_gate * sigmoid_gate
    hidden = silu_gate * pre_up
    hidden_low = hidden.astype(jnp.bfloat16)
    back_proj = jnp.einsum("emd,edf->emf", out_rows, down_full, preferred_element_type=jnp.float32)
    partial_scores = jnp.sum(hidden * back_proj, axis=2)
    scaled = (prob * out_rows.astype(jnp.float32)).astype(jnp.bfloat16)
    hidden_grad = prob * back_proj
    up_grad = (hidden_grad * silu_gate).astype(jnp.bfloat16)
    gate_grad = (
        hidden_grad * pre_up * sigmoid_gate * (1.0 + pre_gate * (1.0 - sigmoid_gate))
    ).astype(jnp.bfloat16)
    input_terms = jnp.einsum(
        "emf,edf->emd", gate_grad, gate_full, preferred_element_type=jnp.float32
    )
    input_terms = input_terms + jnp.einsum(
        "emf,edf->emd", up_grad, up_full, preferred_element_type=jnp.float32
    )
    route_scores = lax.psum(partial_scores, ("tx", "core"))
    input_shards = lax.psum_scatter(
        input_terms.astype(jnp.bfloat16), ("tx", "core"), scatter_dimension=2, tiled=True
    ).astype(jnp.float32)
    back_rows, back_scores = (
        lax.all_to_all(
            by_peer(input_shards).astype(jnp.bfloat16),
            ("expert", "seq"),
            split_axis=0,
            concat_axis=0,
            tiled=True,
        ).astype(jnp.float32),
        lax.all_to_all(
            by_peer(route_scores).astype(jnp.bfloat16),
            ("expert", "seq"),
            split_axis=0,
            concat_axis=0,
            tiled=True,
        ).astype(jnp.float32),
    )
    route_rows = back_rows.reshape(slot_count, part_width)[target].reshape(tok_rows, 2, part_width)
    grad_tokens = jnp.sum(route_rows, axis=1).astype(jnp.bfloat16)
    grad_route = back_scores.reshape(slot_count)[target].reshape(tok_rows, 2)
    gate_part = jnp.einsum("emd,emf->edf", in_rows, gate_grad, preferred_element_type=jnp.float32)
    up_part = jnp.einsum("emd,emf->edf", in_rows, up_grad, preferred_element_type=jnp.float32)
    down_part = jnp.einsum("emd,emf->edf", scaled, hidden_low, preferred_element_type=jnp.float32)
    grad_gate, grad_up, grad_down = (
        lax.psum_scatter(
            gate_part.astype(jnp.bfloat16), "seq", scatter_dimension=1, tiled=True
        ).astype(jnp.float32),
        lax.psum_scatter(
            up_part.astype(jnp.bfloat16), "seq", scatter_dimension=1, tiled=True
        ).astype(jnp.float32),
        lax.psum_scatter(
            down_part.astype(jnp.bfloat16), "seq", scatter_dimension=1, tiled=True
        ).astype(jnp.float32),
    )
    return (grad_tokens, grad_route, grad_gate, grad_up, grad_down)


def solution(mesh):
    shape = mesh.devices.shape
    mesh = jax.sharding.Mesh(
        mesh.devices.reshape(shape[0], shape[1], shape[2] // 2, 2), ("expert", "seq", "tx", "core")
    )
    tensor = ("tx", "core")
    placed = (
        P(("expert", "seq"), None),
        P(("expert", "seq"), None),
        P(("expert", "seq"), None),
        P(("expert", "seq"), None),
        P("expert", "seq", tensor),
        P("expert", "seq", tensor),
        P("expert", "seq", tensor),
    )
    return jax.shard_map(
        shards,
        mesh=mesh,
        in_specs=placed,
        out_specs=(
            P(("expert", "seq"), tensor),
            P(("expert", "seq"), None),
            P("expert", "seq", tensor),
            P("expert", "seq", tensor),
            P("expert", "seq", tensor),
        ),
        check_vma=False,
    )
```

profile of v0, /device:TPU:1, one launch (start us, length us, event | category | flops | bytes accessed | tf_op | source)
XLA Modules:
  0.0 511.5 jit_solution(3057996658511665825)
XLA Ops:
  12.7 2.9 scatter_custom_fusion
  15.7 3.5 gather_fusion
  21.2 4.2 gather_fusion.2
  25.4 4.2 gather_fusion.1
  29.6 6.8 %broadcast_multiply_fusion.1 = (bf16[16,32,3584]{2,1,0:T(8,128)(2,1)}, bf16[16,32,3584]{2,1,0:T(8,128)(2,1)}) fusion(bf16[16,32,3584]{2,1,0:T(8,128)(2,1)} %bitcast.74, bf16[16,32]{1,0:T(8,128)(2,1)S(1)} %reshape.301, bf16[16,32,3584]{2,1,0:T(8,128)(2,1)} %bitcast.73), kind=kLoop, calls=%fused_computation.34 | loop fusion | flops 3670016 | bytes 14681088 | tf_op jit(solution)/shard_map/mul | solution.py:46
  36.4 8.9 %all-to-all-start.2 = ((bf16[16,32,3584]{2,1,0:T(8,128)(2,1)}), bf16[16,32,3584]{2,1,0:T(8,128)(2,1)}, u32[]{:S(2)}, u32[]{:S(2)}) async-start(bf16[16,32,3584]{2,1,0:T(8,128)(2,1)} %get-tuple-element.30), calls=%async_computation.2 | async-start | bytes 7340032 | tf_op jit(solution)/shard_map/all_to_all | solution.py:48
  46.0 70.6 %all-to-all-done.2 = bf16[16,32,3584]{2,1,0:T(8,128)(2,1)} async-done(((bf16[16,32,3584]{2,1,0:T(8,128)(2,1)}), bf16[16,32,3584]{2,1,0:T(8,128)(2,1)}, u32[]{:S(2)}, u32[]{:S(2)}) %all-to-all-start.2) | async-done | bytes 3670048 | tf_op jit(solution)/shard_map/all_to_all | solution.py:48
  118.6 11.5 %all_to_all.31 = bf16[16,1,32]{2,1,0:T(2,128)(2,1)S(1)} all-to-all(bf16[16,1,32]{2,1,0:T(2,128)(2,1)S(1)} %all_to_all.25), channel_id=1, replica_groups=mesh['expert'=4,'seq'=4,'tx'=4,'core'=2] {'expert','seq'}, dimensions={0} | all-to-all | bytes 2048 | tf_op jit(solution)/shard_map/all_to_all | solution.py:50
  130.1 4.5 all-to-all-start.1
  135.5 64.9 %all-to-all-done.1 = bf16[16,32,3584]{2,1,0:T(8,128)(2,1)} async-done(((bf16[16,32,3584]{2,1,0:T(8,128)(2,1)}), bf16[16,32,3584]{2,1,0:T(8,128)(2,1)}, u32[]{:S(2)}, u32[]{:S(2)}) %all-to-all-start.1) | async-done | bytes 3670048 | tf_op jit(solution)/shard_map/all_to_all | solution.py:49
  200.5 6.6 %collective-permute-start = (bf16[16,32,3584]{2,1,0:T(8,128)(2,1)}, bf16[16,32,3584]{2,1,0:T(8,128)(2,1)}, u32[]{:S(2)}, u32[]{:S(2)}) collective-permute-start(bf16[16,32,3584]{2,1,0:T(8,128)(2,1)} %all-to-all-done.1), channel_id=1, source_target_pairs={{0,1},{1,0},{2,3},{3,2},{4,5},{5,4},{6,7},{7,6},{8,9},{9,8},{10,11... | collective-permute-start | bytes 11010056 | tf_op jit(solution)/shard_map/ppermute | solution.py:54
  207.0 5.4 %broadcast_select_fusion.1 = (bf16[16,32,3584]{2,1,0:T(8,128)(2,1)S(1)}, bf16[16,32,3584]{2,1,0:T(8,128)(2,1)}) fusion(bf16[16,32,3584]{2,1,0:T(8,128)(2,1)} %all-to-all-done.2, bf16[16,32,3584]{2,1,0:T(8,128)(2,1)} %collective-permute-done.1, pred[]{:T(512)S(6)} %eq.42), kind=kLoop, calls=%fused_computation.29 | loop fusion | flops 3670016 | bytes 14680065 | tf_op jit(solution)/shard_map/jit(_where)/select_n | solution.py:55
  212.5 5.8 %pad_maximum_fusion.1 = bf16[16,32,7168]{2,1,0:T(8,128)(2,1)} fusion(bf16[16,32,3584]{2,1,0:T(8,128)(2,1)} %get-tuple-element.25, bf16[16,32,3584]{2,1,0:T(8,128)(2,1)S(1)} %get-tuple-element.24), kind=kLoop, calls=%fused_computation.16 | loop fusion | flops 14680064 | bytes 14680064 | tf_op jit(solution)/shard_map/concatenate | solution.py:57
  218.2 6.2 %fusion.7 = f32[512,256]{0,1:T(8,128)S(1)} fusion(bf16[512,7168]{1,0:T(8,128)(2,1)} %bitcast.67, bf16[1,7168,256]{2,1,0:T(8,128)(2,1)} %all-gather.8.cloned.1.call-done), kind=kOutput, calls=%fused_computation.21 | convolution fusion | flops 1879048192 | bytes 11534336 | tf_op jit(solution)/shard_map/emd,edf->emf/dot_general | solution.py:80
  224.5 6.2 %fusion.10 = f32[512,256]{0,1:T(8,128)S(1)} fusion(bf16[512,7168]{1,0:T(8,128)(2,1)} %bitcast.68, bf16[1,7168,256]{2,1,0:T(8,128)(2,1)} %all-gather.6.cloned.1.call-done), kind=kOutput, calls=%fused_computation.24 | convolution fusion | flops 1879048192 | bytes 11534336 | tf_op jit(solution)/shard_map/emd,edf->emf/dot_general | solution.py:81
  230.7 5.6 %broadcast_select_fusion.3 = (bf16[16,32,3584]{2,1,0:T(8,128)(2,1)S(1)}, bf16[16,32,3584]{2,1,0:T(8,128)(2,1)}) fusion(bf16[16,32,3584]{2,1,0:T(8,128)(2,1)} %all-to-all-done.1, bf16[16,32,3584]{2,1,0:T(8,128)(2,1)} %collective-permute-done, pred[]{:T(512)S(6)} %eq.42), kind=kLoop, calls=%fused_computation.31 | loop fusion | flops 3670016 | bytes 14680065 | tf_op jit(solution)/shard_map/jit(_where)/select_n | solution.py:55
  236.3 5.8 %pad_maximum_fusion = bf16[16,32,7168]{2,1,0:T(8,128)(2,1)} fusion(bf16[16,32,3584]{2,1,0:T(8,128)(2,1)} %get-tuple-element.23, bf16[16,32,3584]{2,1,0:T(8,128)(2,1)S(1)} %get-tuple-element.22), kind=kLoop, calls=%fused_computation.15 | loop fusion | flops 14680064 | bytes 14680064 | tf_op jit(solution)/shard_map/concatenate | solution.py:57
  242.1 6.6 %multiply_reduce_fusion = (f32[512]{0:T(512)S(1)}, bf16[512,256]{0,1:T(8,128)(2,1)S(1)}, bf16[512,256]{0,1:T(8,128)(2,1)S(1)}) fusion(f32[512,256]{0,1:T(8,128)S(1)} %fusion.10, f32[512,256]{0,1:T(8,128)S(1)} %fusion.7, f32[512]{0:T(512)S(1)} %reshape.300, bf16[512,7168]{1,0:T(8,128)(2,1)} %bitcast.75, bf16[1,7168,256]{2,1,0:T(8,128)(2,1)} %all-gather.4.cloned.1.call-done), kind=kOutput, calls=%fused_computation.36 | convolution fusion | flops 1881275904 | bytes 12587008 | tf_op jit(solution)/shard_map/emd,edf->emf/dot_general | solution.py:86
  248.7 7.3 %fusion.5 = f32[512,7168]{1,0:T(8,128)} fusion(bf16[512,256]{0,1:T(8,128)(2,1)S(1)} %get-tuple-element.27, bf16[1,7168,256]{2,1,0:T(8,128)(2,1)S(1)} %copy-done.1), kind=kOutput, calls=%fused_computation.19 | convolution fusion | flops 1879048192 | bytes 18612224 | tf_op jit(solution)/shard_map/emf,edf->emd/dot_general | solution.py:94
  256.0 10.6 %fusion = bf16[1,512,7168]{2,1,0:T(8,128)(2,1)} fusion(f32[512,7168]{1,0:T(8,128)} %fusion.5, bf16[512,256]{0,1:T(8,128)(2,1)S(1)} %get-tuple-element.28, bf16[1,7168,256]{2,1,0:T(8,128)(2,1)S(1)} %copy-done), kind=kOutput, calls=%fused_computation.8 | convolution fusion | flops 1886388224 | bytes 25952256 | tf_op jit(solution)/shard_map/emf,edf->emd/dot_general | solution.py:97
  266.6 31.4 %copy.30 = bf16[1,512,7168]{1,0,2:T(2,128)(2,1)} copy(bf16[1,512,7168]{2,1,0:T(8,128)(2,1)} %fusion) | data formatting | bytes 14680064
  298.1 10.3 %copy.36 = bf16[7168,1,512]{2,0,1:T(8,128)(2,1)} copy(bf16[7168,1,512]{2,1,0:T(2,128)(2,1)} %bitcast.71) | data formatting | bytes 14680064
  308.5 8.0 %fusion.3 = bf16[1,7168,256]{2,1,0:T(8,128)(2,1)} fusion(bf16[512,7168]{1,0:T(8,128)(2,1)} %bitcast.76, f32[512]{0:T(512)S(1)} %reshape.300, f32[512,256]{0,1:T(8,128)S(1)} %fusion.10, f32[512,256]{0,1:T(8,128)S(1)} %fusion.7), kind=kOutput, calls=%fused_computation.14 | convolution fusion | flops 1892679680 | bytes 12060672 | tf_op jit(solution)/shard_map/emd,emf->edf/dot_general | solution.py:125
  316.6 7.1 %fusion.1 = bf16[1,7168,256]{2,1,0:T(8,128)(2,1)} fusion(bf16[512,7168]{1,0:T(8,128)(2,1)} %bitcast.69, bf16[512,256]{0,1:T(8,128)(2,1)S(1)} %get-tuple-element.27), kind=kOutput, calls=%fused_computation.12 | convolution fusion | flops 1880883200 | bytes 11272192 | tf_op jit(solution)/shard_map/emd,emf->edf/dot_general | solution.py:123
  323.8 7.2 %fusion.2 = bf16[1,7168,256]{2,1,0:T(8,128)(2,1)} fusion(bf16[512,7168]{1,0:T(8,128)(2,1)} %bitcast.70, bf16[512,256]{0,1:T(8,128)(2,1)S(1)} %get-tuple-element.28), kind=kOutput, calls=%fused_computation.13 | convolution fusion | flops 1880883200 | bytes 11272192 | tf_op jit(solution)/shard_map/emd,emf->edf/dot_general | solution.py:124
  330.9 23.5 %psum.7 = bf16[1,512]{1,0:T(2,128)(2,1)S(1)} all-reduce(f32[1,512]{1,0:T(1,128)S(1)} %bitcast.78), channel_id=1, replica_groups=mesh['expert'=4,'seq'=4,'tx'=4,'core'=2] {'tx','core'}, use_global_device_ids=true, to_apply=%region_7.8 | all-reduce | flops 512 | bytes 3072 | tf_op jit(solution)/shard_map/psum | solution.py:100
  355.1 3.7 all-to-all-start.4
  361.0 3.4 copy.31
  365.1 6.0 %all-to-all-start.3 = ((bf16[16,32,896]{2,1,0:T(8,128)(2,1)}), bf16[16,32,896]{2,1,0:T(8,128)(2,1)S(1)}, u32[]{:S(2)}, u32[]{:S(2)}) async-start(bf16[16,32,896]{2,1,0:T(8,128)(2,1)} %bitcast.9), calls=%async_computation.3 | async-start | bytes 1835008 | tf_op jit(solution)/shard_map/all_to_all | solution.py:105
  374.8 32.5 %reduce-scatter.11.cloned.1.call-done = bf16[1,1792,256]{2,1,0:T(8,128)(2,1)} async-done(((bf16[1,7168,256]{2,1,0:T(8,128)(2,1)}), bf16[1,1792,256]{2,1,0:T(8,128)(2,1)}) %reduce-scatter.11.cloned.1.call-update) | async-done | bytes 917520 | tf_op jit(solution)/shard_map/reduce_scatter | solution.py:133
  409.9 41.9 %reduce-scatter.7.cloned.1.call-done = bf16[1,1792,256]{2,1,0:T(8,128)(2,1)} async-done(((bf16[1,7168,256]{2,1,0:T(8,128)(2,1)}), bf16[1,1792,256]{2,1,0:T(8,128)(2,1)}) %reduce-scatter.7.cloned.1.call-update) | async-done | bytes 917520 | tf_op jit(solution)/shard_map/reduce_scatter | solution.py:127
  454.3 42.1 %reduce-scatter.9.cloned.1.call-done = bf16[1,1792,256]{2,1,0:T(8,128)(2,1)} async-done(((bf16[1,7168,256]{2,1,0:T(8,128)(2,1)}), bf16[1,1792,256]{2,1,0:T(8,128)(2,1)}) %reduce-scatter.9.cloned.1.call-update) | async-done | bytes 917520 | tf_op jit(solution)/shard_map/reduce_scatter | solution.py:130
  (68 shorter events, 31.6 us)
Async XLA Ops:
  7.2 211.1 %all-gather.8.cloned.1.call-start = ((), (), s32[]{:S(2)}) async-start(), calls=%async_computation.11 | async-start | bytes 4587520 | tf_op jit(solution)/shard_map/all_gather | solution.py:76
  36.4 80.3 %all-to-all-start.2 = ((bf16[16,32,3584]{2,1,0:T(8,128)(2,1)}), bf16[16,32,3584]{2,1,0:T(8,128)(2,1)}, u32[]{:S(2)}, u32[]{:S(2)}) async-start(bf16[16,32,3584]{2,1,0:T(8,128)(2,1)} %get-tuple-element.30), calls=%async_computation.2 | async-start | bytes 7340032 | tf_op jit(solution)/shard_map/all_to_all | solution.py:48
  45.3 179.2 %all-gather.6.cloned.1.call-start = ((), (), s32[]{:S(2)}) async-start(), calls=%async_computation.10 | async-start | bytes 4587520 | tf_op jit(solution)/shard_map/all_gather | solution.py:77
  116.7 90.4 %collective-permute-start.1 = (bf16[16,32,3584]{2,1,0:T(8,128)(2,1)}, bf16[16,32,3584]{2,1,0:T(8,128)(2,1)}, u32[]{:S(2)}, u32[]{:S(2)}) collective-permute-start(bf16[16,32,3584]{2,1,0:T(8,128)(2,1)} %all-to-all-done.2), channel_id=1, source_target_pairs={{0,1},{1,0},{2,3},{3,2},{4,5},{5,4},{6,7},{7,6},{8,9},{9,8},{10,11... | collective-permute-start | bytes 11010056 | tf_op jit(solution)/shard_map/ppermute | solution.py:54
  130.1 70.3 %all-to-all-start.1 = ((bf16[16,32,3584]{2,1,0:T(8,128)(2,1)}), bf16[16,32,3584]{2,1,0:T(8,128)(2,1)}, u32[]{:S(2)}, u32[]{:S(2)}) async-start(bf16[16,32,3584]{2,1,0:T(8,128)(2,1)} %get-tuple-element.29), calls=%async_computation.1 | async-start | bytes 7340032 | tf_op jit(solution)/shard_map/all_to_all | solution.py:49
  134.6 107.4 %all-gather.4.cloned.1.call-start = ((), (), s32[]{:S(2)}) async-start(), calls=%async_computation.9 | async-start | bytes 4587520 | tf_op jit(solution)/shard_map/all_gather | solution.py:78
  135.4 223.5 %reduce-scatter.13.cloned.1.call-start = ((), (), s32[]{:S(2)}) async-start(), calls=%async_computation.15 | async-start | bytes 8257536
  200.5 30.3 %collective-permute-start = (bf16[16,32,3584]{2,1,0:T(8,128)(2,1)}, bf16[16,32,3584]{2,1,0:T(8,128)(2,1)}, u32[]{:S(2)}, u32[]{:S(2)}) collective-permute-start(bf16[16,32,3584]{2,1,0:T(8,128)(2,1)} %all-to-all-done.1), channel_id=1, source_target_pairs={{0,1},{1,0},{2,3},{3,2},{4,5},{5,4},{6,7},{7,6},{8,9},{9,8},{10,11... | collective-permute-start | bytes 11010056 | tf_op jit(solution)/shard_map/ppermute | solution.py:54
  242.1 6.6 %copy-start.1 = (bf16[1,7168,256]{2,1,0:T(8,128)(2,1)S(1)}, bf16[1,7168,256]{2,1,0:T(8,128)(2,1)}, u32[]{:S(2)}) copy-start(bf16[1,7168,256]{2,1,0:T(8,128)(2,1)} %all-gather.8.cloned.1.call-done) | copy-start | bytes 11010052
  248.7 7.4 %copy-start = (bf16[1,7168,256]{2,1,0:T(8,128)(2,1)S(1)}, bf16[1,7168,256]{2,1,0:T(8,128)(2,1)}, u32[]{:S(2)}) copy-start(bf16[1,7168,256]{2,1,0:T(8,128)(2,1)} %all-gather.6.cloned.1.call-done) | copy-start | bytes 11010052
  308.4 98.9 %reduce-scatter.11.cloned.1.call-start = ((), (), s32[]{:S(2)}) async-start(), calls=%async_computation.14 | async-start | bytes 4587520 | tf_op jit(solution)/shard_map/reduce_scatter | solution.py:133
  316.5 135.2 %reduce-scatter.7.cloned.1.call-start = ((), (), s32[]{:S(2)}) async-start(), calls=%async_computation.12 | async-start | bytes 4587520 | tf_op jit(solution)/shard_map/reduce_scatter | solution.py:127
  323.7 172.7 %reduce-scatter.9.cloned.1.call-start = ((), (), s32[]{:S(2)}) async-start(), calls=%async_computation.13 | async-start | bytes 4587520 | tf_op jit(solution)/shard_map/reduce_scatter | solution.py:130
  355.1 9.9 %all-to-all-start.4 = ((bf16[16,1,32]{2,1,0:T(2,128)(2,1)}), bf16[16,1,32]{2,1,0:T(2,128)(2,1)S(1)}, u32[]{:S(2)}, u32[]{:S(2)}) async-start(bf16[16,1,32]{2,1,0:T(2,128)(2,1)} %convert_element_type.144), calls=%async_computation.4 | async-start | bytes 16384 | tf_op jit(solution)/shard_map/all_to_all | solution.py:112
  365.1 133.9 %all-to-all-start.3 = ((bf16[16,32,896]{2,1,0:T(8,128)(2,1)}), bf16[16,32,896]{2,1,0:T(8,128)(2,1)S(1)}, u32[]{:S(2)}, u32[]{:S(2)}) async-start(bf16[16,32,896]{2,1,0:T(8,128)(2,1)} %bitcast.9), calls=%async_computation.3 | async-start | bytes 1835008 | tf_op jit(solution)/shard_map/all_to_all | solution.py:105
Sparse Core Ops, SparseCore 0:
  9.7 68.7 all-gather.7
  80.2 55.4 all-gather.5
  137.3 70.2 all-gather.3
  308.6 43.6 reduce-scatter.12
  354.5 52.7 reduce-scatter.10
  409.6 42.1 reduce-scatter.6
  454.2 42.2 reduce-scatter.8
where the time goes:
time: 519 us; the launch traced here: 512 us
  waiting for transfers between devices  255 us (49%)
  local copies, waits for them, and re-layouts  73.9 us (14%)
  matrix products  59.3 us (11%)
  other arithmetic  42 us (8%)
  blocking collectives  35 us (7%)
  starting transfers between devices  31.7 us (6%)
  between operations  14.6 us (3%)
    all_to_all x1, waiting for transfers between devices, shards(): lax.all_to_all(in_send, ('expert', 'seq'), split_axis=0, concat_axis=0, t...  70.6 us
    all_to_all x1, waiting for transfers between devices, shards(): lax.all_to_all(out_send, ('expert', 'seq'), split_axis=0, concat_axis=0,...  64.9 us
    unnamed x11, local copies, waits for them, and re-layouts  49.6 us
    reduce_scatter x1, waiting for transfers between devices, shards(): lax.psum_scatter(up_part.astype(jnp.bfloat16), 'seq', scatter_dimension=1...  42.1 us
    reduce_scatter x1, waiting for transfers between devices, shards(): lax.psum_scatter(gate_part.astype(jnp.bfloat16), 'seq', scatter_dimension...  41.9 us
    reduce_scatter x1, waiting for transfers between devices, shards(): lax.psum_scatter(down_part.astype(jnp.bfloat16), 'seq', scatter_dimension...  32.5 us
    psum x1, blocking collectives, shards(): route_scores = lax.psum(partial_scores, ('tx', 'core'))  23.5 us
    all_to_all x1, blocking collectives, shards(): lax.all_to_all(weight_send, ('expert', 'seq'), split_axis=0, concat_axis=...  11.5 us
  transfers between devices with their start and end apart: 13, of which 6 were waited for; matrix products, arithmetic and copies ran while one was open for 20% of the time, Pallas kernels for 0%

commit v1 on v0

--- a/solution.py
+++ b/solution.py
@@ -97,7 +97,7 @@
     input_terms = input_terms + jnp.einsum(
         "emf,edf->emd", up_grad, up_full, preferred_element_type=jnp.float32
     )
-    route_scores = lax.psum(partial_scores, ("tx", "core"))
+    route_scores = lax.psum(lax.psum(partial_scores, "core"), "tx")
     input_shards = lax.psum_scatter(
         input_terms.astype(jnp.bfloat16), ("tx", "core"), scatter_dimension=2, tiled=True
     ).astype(jnp.float32)

time: 519 us -> 519 us (level)
  blocking collectives: 35 us -> 28.7 us
  waiting for transfers between devices: 255 us -> 261 us
    psum x1 -> x2, blocking collectives: 23.5 us -> 17.1 us  [shards(): route_scores = lax.psum(lax.psum(partial_scores, 'core'), 'tx')]
    reduce_scatter x1, waiting for transfers between devices: 32.5 us -> 38.7 us  [shards(): lax.psum_scatter(down_part.astype(jnp.bfloat16), 'seq', scatter_dimension...]
where the time goes in v1:
time: 519 us; the launch traced here: 511 us
  waiting for transfers between devices  261 us (50%)
  local copies, waits for them, and re-layouts  73.9 us (14%)
  matrix products  59.3 us (11%)
  other arithmetic  42 us (8%)
  starting transfers between devices  31.7 us (6%)
  blocking collectives  28.7 us (6%)
  between operations  14.6 us (3%)
    all_to_all x1, waiting for transfers between devices, shards(): lax.all_to_all(in_send, ('expert', 'seq'), split_axis=0, concat_axis=0, t...  70.6 us
    all_to_all x1, waiting for transfers between devices, shards(): lax.all_to_all(out_send, ('expert', 'seq'), split_axis=0, concat_axis=0,...  64.9 us
    unnamed x11, local copies, waits for them, and re-layouts  49.6 us
    reduce_scatter x1, waiting for transfers between devices, shards(): lax.psum_scatter(up_part.astype(jnp.bfloat16), 'seq', scatter_dimension=1...  42.1 us
    reduce_scatter x1, waiting for transfers between devices, shards(): lax.psum_scatter(gate_part.astype(jnp.bfloat16), 'seq', scatter_dimension...  42 us
    reduce_scatter x1, waiting for transfers between devices, shards(): lax.psum_scatter(down_part.astype(jnp.bfloat16), 'seq', scatter_dimension...  38.7 us
    psum x2, blocking collectives, shards(): route_scores = lax.psum(lax.psum(partial_scores, 'core'), 'tx')  17.1 us
    all_to_all x1, blocking collectives, shards(): lax.all_to_all(weight_send, ('expert', 'seq'), split_axis=0, concat_axis=...  11.5 us
  transfers between devices with their start and end apart: 13, of which 6 were waited for; matrix products, arithmetic and copies ran while one was open for 20% of the time, Pallas kernels for 0%

profile of v1, /device:TPU:1, one launch (start us, length us, event | category | flops | bytes accessed | tf_op | source)
XLA Modules:
  0.0 511.4 jit_solution(2117565139440539300)
XLA Ops:
  12.7 2.9 scatter_custom_fusion
  15.7 3.5 gather_fusion
  21.2 4.2 gather_fusion.2
  25.4 4.2 gather_fusion.1
  29.6 6.8 %broadcast_multiply_fusion.1 = (bf16[16,32,3584]{2,1,0:T(8,128)(2,1)}, bf16[16,32,3584]{2,1,0:T(8,128)(2,1)}) fusion(bf16[16,32,3584]{2,1,0:T(8,128)(2,1)} %bitcast.74, bf16[16,32]{1,0:T(8,128)(2,1)S(1)} %reshape.301, bf16[16,32,3584]{2,1,0:T(8,128)(2,1)} %bitcast.73), kind=kLoop, calls=%fused_computation.34 | loop fusion | flops 3670016 | bytes 14681088 | tf_op jit(solution)/shard_map/mul | solution.py:46
  36.4 8.9 %all-to-all-start.2 = ((bf16[16,32,3584]{2,1,0:T(8,128)(2,1)}), bf16[16,32,3584]{2,1,0:T(8,128)(2,1)}, u32[]{:S(2)}, u32[]{:S(2)}) async-start(bf16[16,32,3584]{2,1,0:T(8,128)(2,1)} %get-tuple-element.30), calls=%async_computation.2 | async-start | bytes 7340032 | tf_op jit(solution)/shard_map/all_to_all | solution.py:48
  46.0 70.6 %all-to-all-done.2 = bf16[16,32,3584]{2,1,0:T(8,128)(2,1)} async-done(((bf16[16,32,3584]{2,1,0:T(8,128)(2,1)}), bf16[16,32,3584]{2,1,0:T(8,128)(2,1)}, u32[]{:S(2)}, u32[]{:S(2)}) %all-to-all-start.2) | async-done | bytes 3670048 | tf_op jit(solution)/shard_map/all_to_all | solution.py:48
  118.6 11.5 %all_to_all.31 = bf16[16,1,32]{2,1,0:T(2,128)(2,1)S(1)} all-to-all(bf16[16,1,32]{2,1,0:T(2,128)(2,1)S(1)} %all_to_all.25), channel_id=1, replica_groups=mesh['expert'=4,'seq'=4,'tx'=4,'core'=2] {'expert','seq'}, dimensions={0} | all-to-all | bytes 2048 | tf_op jit(solution)/shard_map/all_to_all | solution.py:50
  130.1 4.5 all-to-all-start.1
  135.5 64.9 %all-to-all-done.1 = bf16[16,32,3584]{2,1,0:T(8,128)(2,1)} async-done(((bf16[16,32,3584]{2,1,0:T(8,128)(2,1)}), bf16[16,32,3584]{2,1,0:T(8,128)(2,1)}, u32[]{:S(2)}, u32[]{:S(2)}) %all-to-all-start.1) | async-done | bytes 3670048 | tf_op jit(solution)/shard_map/all_to_all | solution.py:49
  200.5 6.6 %collective-permute-start = (bf16[16,32,3584]{2,1,0:T(8,128)(2,1)}, bf16[16,32,3584]{2,1,0:T(8,128)(2,1)}, u32[]{:S(2)}, u32[]{:S(2)}) collective-permute-start(bf16[16,32,3584]{2,1,0:T(8,128)(2,1)} %all-to-all-done.1), channel_id=1, source_target_pairs={{0,1},{1,0},{2,3},{3,2},{4,5},{5,4},{6,7},{7,6},{8,9},{9,8},{10,11... | collective-permute-start | bytes 11010056 | tf_op jit(solution)/shard_map/ppermute | solution.py:54
  207.0 5.4 %broadcast_select_fusion.1 = (bf16[16,32,3584]{2,1,0:T(8,128)(2,1)S(1)}, bf16[16,32,3584]{2,1,0:T(8,128)(2,1)}) fusion(bf16[16,32,3584]{2,1,0:T(8,128)(2,1)} %all-to-all-done.2, bf16[16,32,3584]{2,1,0:T(8,128)(2,1)} %collective-permute-done.1, pred[]{:T(512)S(6)} %eq.42), kind=kLoop, calls=%fused_computation.29 | loop fusion | flops 3670016 | bytes 14680065 | tf_op jit(solution)/shard_map/jit(_where)/select_n | solution.py:55
  212.5 5.8 %pad_maximum_fusion.1 = bf16[16,32,7168]{2,1,0:T(8,128)(2,1)} fusion(bf16[16,32,3584]{2,1,0:T(8,128)(2,1)} %get-tuple-element.25, bf16[16,32,3584]{2,1,0:T(8,128)(2,1)S(1)} %get-tuple-element.24), kind=kLoop, calls=%fused_computation.16 | loop fusion | flops 14680064 | bytes 14680064 | tf_op jit(solution)/shard_map/concatenate | solution.py:57
  218.2 6.2 %fusion.7 = f32[512,256]{0,1:T(8,128)S(1)} fusion(bf16[512,7168]{1,0:T(8,128)(2,1)} %bitcast.67, bf16[1,7168,256]{2,1,0:T(8,128)(2,1)} %all-gather.8.cloned.1.call-done), kind=kOutput, calls=%fused_computation.21 | convolution fusion | flops 1879048192 | bytes 11534336 | tf_op jit(solution)/shard_map/emd,edf->emf/dot_general | solution.py:80
  224.5 6.2 %fusion.10 = f32[512,256]{0,1:T(8,128)S(1)} fusion(bf16[512,7168]{1,0:T(8,128)(2,1)} %bitcast.68, bf16[1,7168,256]{2,1,0:T(8,128)(2,1)} %all-gather.6.cloned.1.call-done), kind=kOutput, calls=%fused_computation.24 | convolution fusion | flops 1879048192 | bytes 11534336 | tf_op jit(solution)/shard_map/emd,edf->emf/dot_general | solution.py:81
  230.7 5.6 %broadcast_select_fusion.3 = (bf16[16,32,3584]{2,1,0:T(8,128)(2,1)S(1)}, bf16[16,32,3584]{2,1,0:T(8,128)(2,1)}) fusion(bf16[16,32,3584]{2,1,0:T(8,128)(2,1)} %all-to-all-done.1, bf16[16,32,3584]{2,1,0:T(8,128)(2,1)} %collective-permute-done, pred[]{:T(512)S(6)} %eq.42), kind=kLoop, calls=%fused_computation.31 | loop fusion | flops 3670016 | bytes 14680065 | tf_op jit(solution)/shard_map/jit(_where)/select_n | solution.py:55
  236.3 5.8 %pad_maximum_fusion = bf16[16,32,7168]{2,1,0:T(8,128)(2,1)} fusion(bf16[16,32,3584]{2,1,0:T(8,128)(2,1)} %get-tuple-element.23, bf16[16,32,3584]{2,1,0:T(8,128)(2,1)S(1)} %get-tuple-element.22), kind=kLoop, calls=%fused_computation.15 | loop fusion | flops 14680064 | bytes 14680064 | tf_op jit(solution)/shard_map/concatenate | solution.py:57
  242.1 6.6 %multiply_reduce_fusion = (f32[512]{0:T(512)S(1)}, bf16[512,256]{0,1:T(8,128)(2,1)S(1)}, bf16[512,256]{0,1:T(8,128)(2,1)S(1)}) fusion(f32[512,256]{0,1:T(8,128)S(1)} %fusion.10, f32[512,256]{0,1:T(8,128)S(1)} %fusion.7, f32[512]{0:T(512)S(1)} %reshape.300, bf16[512,7168]{1,0:T(8,128)(2,1)} %bitcast.75, bf16[1,7168,256]{2,1,0:T(8,128)(2,1)} %all-gather.4.cloned.1.call-done), kind=kOutput, calls=%fused_computation.36 | convolution fusion | flops 1881275904 | bytes 12587008 | tf_op jit(solution)/shard_map/emd,edf->emf/dot_general | solution.py:86
  248.7 7.3 %fusion.5 = f32[512,7168]{1,0:T(8,128)} fusion(bf16[512,256]{0,1:T(8,128)(2,1)S(1)} %get-tuple-element.27, bf16[1,7168,256]{2,1,0:T(8,128)(2,1)S(1)} %copy-done.1), kind=kOutput, calls=%fused_computation.19 | convolution fusion | flops 1879048192 | bytes 18612224 | tf_op jit(solution)/shard_map/emf,edf->emd/dot_general | solution.py:94
  256.0 10.6 %fusion = bf16[1,512,7168]{2,1,0:T(8,128)(2,1)} fusion(f32[512,7168]{1,0:T(8,128)} %fusion.5, bf16[512,256]{0,1:T(8,128)(2,1)S(1)} %get-tuple-element.28, bf16[1,7168,256]{2,1,0:T(8,128)(2,1)S(1)} %copy-done), kind=kOutput, calls=%fused_computation.8 | convolution fusion | flops 1886388224 | bytes 25952256 | tf_op jit(solution)/shard_map/emf,edf->emd/dot_general | solution.py:97
  266.6 31.4 %copy.30 = bf16[1,512,7168]{1,0,2:T(2,128)(2,1)} copy(bf16[1,512,7168]{2,1,0:T(8,128)(2,1)} %fusion) | data formatting | bytes 14680064
  298.1 10.3 %copy.36 = bf16[7168,1,512]{2,0,1:T(8,128)(2,1)} copy(bf16[7168,1,512]{2,1,0:T(2,128)(2,1)} %bitcast.71) | data formatting | bytes 14680064
  308.5 8.0 %fusion.3 = bf16[1,7168,256]{2,1,0:T(8,128)(2,1)} fusion(bf16[512,7168]{1,0:T(8,128)(2,1)} %bitcast.76, f32[512]{0:T(512)S(1)} %reshape.300, f32[512,256]{0,1:T(8,128)S(1)} %fusion.10, f32[512,256]{0,1:T(8,128)S(1)} %fusion.7), kind=kOutput, calls=%fused_computation.14 | convolution fusion | flops 1892679680 | bytes 12060672 | tf_op jit(solution)/shard_map/emd,emf->edf/dot_general | solution.py:125
  316.6 7.1 %fusion.1 = bf16[1,7168,256]{2,1,0:T(8,128)(2,1)} fusion(bf16[512,7168]{1,0:T(8,128)(2,1)} %bitcast.69, bf16[512,256]{0,1:T(8,128)(2,1)S(1)} %get-tuple-element.27), kind=kOutput, calls=%fused_computation.12 | convolution fusion | flops 1880883200 | bytes 11272192 | tf_op jit(solution)/shard_map/emd,emf->edf/dot_general | solution.py:123
  323.8 7.2 %fusion.2 = bf16[1,7168,256]{2,1,0:T(8,128)(2,1)} fusion(bf16[512,7168]{1,0:T(8,128)(2,1)} %bitcast.70, bf16[512,256]{0,1:T(8,128)(2,1)S(1)} %get-tuple-element.28), kind=kOutput, calls=%fused_computation.13 | convolution fusion | flops 1880883200 | bytes 11272192 | tf_op jit(solution)/shard_map/emd,emf->edf/dot_general | solution.py:124
  333.4 14.7 %psum.15 = bf16[1,512]{1,0:T(2,128)(2,1)S(1)} all-reduce(f32[1,512]{1,0:T(1,128)S(1)} %psum.14), channel_id=1, replica_groups=mesh['expert'=4,'seq'=4,'tx'=4,'core'=2] {'tx'}, use_global_device_ids=true, to_apply=%region_8.9 | all-reduce | flops 512 | bytes 3072 | tf_op jit(solution)/shard_map/psum | solution.py:100
  348.8 3.7 all-to-all-start.4
  354.6 3.4 copy.31
  358.7 6.0 %all-to-all-start.3 = ((bf16[16,32,896]{2,1,0:T(8,128)(2,1)}), bf16[16,32,896]{2,1,0:T(8,128)(2,1)S(1)}, u32[]{:S(2)}, u32[]{:S(2)}) async-start(bf16[16,32,896]{2,1,0:T(8,128)(2,1)} %bitcast.9), calls=%async_computation.3 | async-start | bytes 1835008 | tf_op jit(solution)/shard_map/all_to_all | solution.py:105
  368.5 38.7 %reduce-scatter.11.cloned.1.call-done = bf16[1,1792,256]{2,1,0:T(8,128)(2,1)} async-done(((bf16[1,7168,256]{2,1,0:T(8,128)(2,1)}), bf16[1,1792,256]{2,1,0:T(8,128)(2,1)}) %reduce-scatter.11.cloned.1.call-update) | async-done | bytes 917520 | tf_op jit(solution)/shard_map/reduce_scatter | solution.py:133
  409.7 42.0 %reduce-scatter.7.cloned.1.call-done = bf16[1,1792,256]{2,1,0:T(8,128)(2,1)} async-done(((bf16[1,7168,256]{2,1,0:T(8,128)(2,1)}), bf16[1,1792,256]{2,1,0:T(8,128)(2,1)}) %reduce-scatter.7.cloned.1.call-update) | async-done | bytes 917520 | tf_op jit(solution)/shard_map/reduce_scatter | solution.py:127
  454.2 42.1 %reduce-scatter.9.cloned.1.call-done = bf16[1,1792,256]{2,1,0:T(8,128)(2,1)} async-done(((bf16[1,7168,256]{2,1,0:T(8,128)(2,1)}), bf16[1,1792,256]{2,1,0:T(8,128)(2,1)}) %reduce-scatter.9.cloned.1.call-update) | async-done | bytes 917520 | tf_op jit(solution)/shard_map/reduce_scatter | solution.py:130
  (69 shorter events, 34.1 us)
Async XLA Ops:
  7.2 211.1 %all-gather.8.cloned.1.call-start = ((), (), s32[]{:S(2)}) async-start(), calls=%async_computation.11 | async-start | bytes 4587520 | tf_op jit(solution)/shard_map/all_gather | solution.py:76
  36.4 80.3 %all-to-all-start.2 = ((bf16[16,32,3584]{2,1,0:T(8,128)(2,1)}), bf16[16,32,3584]{2,1,0:T(8,128)(2,1)}, u32[]{:S(2)}, u32[]{:S(2)}) async-start(bf16[16,32,3584]{2,1,0:T(8,128)(2,1)} %get-tuple-element.30), calls=%async_computation.2 | async-start | bytes 7340032 | tf_op jit(solution)/shard_map/all_to_all | solution.py:48
  45.3 179.2 %all-gather.6.cloned.1.call-start = ((), (), s32[]{:S(2)}) async-start(), calls=%async_computation.10 | async-start | bytes 4587520 | tf_op jit(solution)/shard_map/all_gather | solution.py:77
  116.7 90.4 %collective-permute-start.1 = (bf16[16,32,3584]{2,1,0:T(8,128)(2,1)}, bf16[16,32,3584]{2,1,0:T(8,128)(2,1)}, u32[]{:S(2)}, u32[]{:S(2)}) collective-permute-start(bf16[16,32,3584]{2,1,0:T(8,128)(2,1)} %all-to-all-done.2), channel_id=1, source_target_pairs={{0,1},{1,0},{2,3},{3,2},{4,5},{5,4},{6,7},{7,6},{8,9},{9,8},{10,11... | collective-permute-start | bytes 11010056 | tf_op jit(solution)/shard_map/ppermute | solution.py:54
  130.1 70.3 %all-to-all-start.1 = ((bf16[16,32,3584]{2,1,0:T(8,128)(2,1)}), bf16[16,32,3584]{2,1,0:T(8,128)(2,1)}, u32[]{:S(2)}, u32[]{:S(2)}) async-start(bf16[16,32,3584]{2,1,0:T(8,128)(2,1)} %get-tuple-element.29), calls=%async_computation.1 | async-start | bytes 7340032 | tf_op jit(solution)/shard_map/all_to_all | solution.py:49
  134.6 107.4 %all-gather.4.cloned.1.call-start = ((), (), s32[]{:S(2)}) async-start(), calls=%async_computation.9 | async-start | bytes 4587520 | tf_op jit(solution)/shard_map/all_gather | solution.py:78
  135.4 217.1 %reduce-scatter.13.cloned.1.call-start = ((), (), s32[]{:S(2)}) async-start(), calls=%async_computation.15 | async-start | bytes 8257536
  200.5 30.3 %collective-permute-start = (bf16[16,32,3584]{2,1,0:T(8,128)(2,1)}, bf16[16,32,3584]{2,1,0:T(8,128)(2,1)}, u32[]{:S(2)}, u32[]{:S(2)}) collective-permute-start(bf16[16,32,3584]{2,1,0:T(8,128)(2,1)} %all-to-all-done.1), channel_id=1, source_target_pairs={{0,1},{1,0},{2,3},{3,2},{4,5},{5,4},{6,7},{7,6},{8,9},{9,8},{10,11... | collective-permute-start | bytes 11010056 | tf_op jit(solution)/shard_map/ppermute | solution.py:54
  242.1 6.6 %copy-start.1 = (bf16[1,7168,256]{2,1,0:T(8,128)(2,1)S(1)}, bf16[1,7168,256]{2,1,0:T(8,128)(2,1)}, u32[]{:S(2)}) copy-start(bf16[1,7168,256]{2,1,0:T(8,128)(2,1)} %all-gather.8.cloned.1.call-done) | copy-start | bytes 11010052
  248.7 7.4 %copy-start = (bf16[1,7168,256]{2,1,0:T(8,128)(2,1)S(1)}, bf16[1,7168,256]{2,1,0:T(8,128)(2,1)}, u32[]{:S(2)}) copy-start(bf16[1,7168,256]{2,1,0:T(8,128)(2,1)} %all-gather.6.cloned.1.call-done) | copy-start | bytes 11010052
  308.4 98.7 %reduce-scatter.11.cloned.1.call-start = ((), (), s32[]{:S(2)}) async-start(), calls=%async_computation.14 | async-start | bytes 4587520 | tf_op jit(solution)/shard_map/reduce_scatter | solution.py:133
  316.5 135.2 %reduce-scatter.7.cloned.1.call-start = ((), (), s32[]{:S(2)}) async-start(), calls=%async_computation.12 | async-start | bytes 4587520 | tf_op jit(solution)/shard_map/reduce_scatter | solution.py:127
  323.7 172.6 %reduce-scatter.9.cloned.1.call-start = ((), (), s32[]{:S(2)}) async-start(), calls=%async_computation.13 | async-start | bytes 4587520 | tf_op jit(solution)/shard_map/reduce_scatter | solution.py:130
  348.8 9.9 %all-to-all-start.4 = ((bf16[16,1,32]{2,1,0:T(2,128)(2,1)}), bf16[16,1,32]{2,1,0:T(2,128)(2,1)S(1)}, u32[]{:S(2)}, u32[]{:S(2)}) async-start(bf16[16,1,32]{2,1,0:T(2,128)(2,1)} %convert_element_type.144), calls=%async_computation.4 | async-start | bytes 16384 | tf_op jit(solution)/shard_map/all_to_all | solution.py:112
  358.7 140.2 %all-to-all-start.3 = ((bf16[16,32,896]{2,1,0:T(8,128)(2,1)}), bf16[16,32,896]{2,1,0:T(8,128)(2,1)S(1)}, u32[]{:S(2)}, u32[]{:S(2)}) async-start(bf16[16,32,896]{2,1,0:T(8,128)(2,1)} %bitcast.9), calls=%async_computation.3 | async-start | bytes 1835008 | tf_op jit(solution)/shard_map/all_to_all | solution.py:105
Sparse Core Ops, SparseCore 0:
  9.7 68.7 all-gather.7
  80.2 55.4 all-gather.5
  137.3 70.2 all-gather.3
  308.6 43.6 reduce-scatter.12
  354.5 52.5 reduce-scatter.10
  409.4 42.2 reduce-scatter.6
  454.1 42.2 reduce-scatter.8
